TPU v7x, 32 devices: a whole 2x2x4 slice. The times are simulated.
32 devices in a mesh: task: 4 (over z), feat: 8 (over y, x, core).
Axes of the slice: x: 2, y: 2, z: 4, core: 2. Of those that a mesh axis runs over, the one named last changes fastest.
Arguments:
- inputs: bfloat16 [4, 64, 512, 512], P('task', 'feat'), may hold values from -6 to 6
- context: int32 [4], P('task'), may hold values from 50 to 500, as said below
- sample_mask: int32 [4, 512], P('task'), may hold values from 0 to 1, as said below
- sample_gain: float32 [512], replicated, may hold values from 0.5 to 1.5
- sample_shift: float32 [512], replicated, may hold values from -2 to 2
- sample_project: bfloat16 [512, 1536], replicated, may hold values from -0.25 to 0.25
- sample_output: bfloat16 [512, 512], replicated, may hold values from -1 to 1
- sample_bias: float32 [512], replicated, may hold values from -2 to 2
- feature_gain: float32 [512], replicated, may hold values from 0.5 to 1.5
- feature_shift: float32 [512], replicated, may hold values from -2 to 2
- feature_project: bfloat16 [512, 1536], replicated, may hold values from -0.25 to 0.25
- feature_output: bfloat16 [512, 512], replicated, may hold values from -0.75 to 0.75
- feature_bias: float32 [512], replicated, may hold values from -2 to 2
- dense_gain: float32 [512], replicated, may hold values from 0.5 to 1.5
- dense_shift: float32 [512], replicated, may hold values from -2 to 2
- up_weight: bfloat16 [512, 2048], replicated, may hold values from -0.25 to 0.25
- up_bias: float32 [2048], replicated, may hold values from -2 to 2
- down_weight: bfloat16 [2048, 512], replicated, may hold values from -0.125 to 0.125
- down_bias: float32 [512], replicated, may hold values from -2 to 2
- cotangent: bfloat16 [4, 64, 512, 512], P('task', 'feat'), may hold values from -6 to 6
Outputs:
- output: bfloat16 [4, 64, 512, 512], P('task', 'feat')
- input_grad: float32 [4, 64, 512, 512], P('task', 'feat')
- sample_gain_grad: float32 [512], replicated
- sample_shift_grad: float32 [512], replicated
- sample_project_grad: float32 [512, 1536], replicated
- sample_output_grad: float32 [512, 512], replicated
- sample_bias_grad: float32 [512], replicated
- feature_gain_grad: float32 [512], replicated
- feature_shift_grad: float32 [512], replicated
- feature_project_grad: float32 [512, 1536], replicated
- feature_output_grad: float32 [512, 512], replicated
- feature_bias_grad: float32 [512], replicated
- dense_gain_grad: float32 [512], replicated
- dense_shift_grad: float32 [512], replicated
- up_weight_grad: float32 [512, 2048], replicated
- up_bias_grad: float32 [2048], replicated
- down_weight_grad: float32 [2048, 512], replicated
- down_bias_grad: float32 [512], replicated
Inputs may be any that keep to these rules, and one draw needn't show every extreme that they name: In every draw one task has context 50 and another 500. `sample_mask`: sample 0 of every task is present.
All inputs are finite; a program needn't handle non-finite values.
Results may differ from a plain program's by a relative error of at most 0.015.
Values may be sent and summed in bfloat16 or wider, within the bound.
A program may use at most 384 MiB of HBM per device.

v0:
```python
import jax
import jax.numpy as jnp
from jax import lax
from jax.sharding import PartitionSpec as P

HEADS = 8
HEAD = 64
EPSILON = 1e-05


def norm_apply(token_rows, norm_gain, norm_shift):
    center = token_rows - jnp.mean(token_rows, axis=-1, keepdims=True)
    spread = jnp.mean(center * center, axis=-1, keepdims=True)
    return center * lax.rsqrt(spread + EPSILON) * norm_gain + norm_shift


def attend_block(queries, key_rows, values, visible):
    scores = jnp.einsum(
        "qche,kche->chqk", queries, key_rows, preferred_element_type=jnp.float32
    ) * HEAD ** (-0.5)
    scores = jnp.where(visible, scores, -1e30)
    highest = jnp.max(scores, axis=-1, keepdims=True)
    weights = jnp.exp(scores - highest)
    totals = jnp.sum(weights, axis=-1, keepdims=True)
    shares = (weights / totals).astype(jnp.bfloat16)
    mixed = jnp.einsum("chqk,kche->qche", shares, values, preferred_element_type=jnp.float32)
    return (mixed.astype(jnp.bfloat16), highest[..., 0] + jnp.log(totals[..., 0]))


def attend_back(queries, key_rows, values, visible, log_total, grad_mixed):
    scores = jnp.einsum(
        "qche,kche->chqk", queries, key_rows, preferred_element_type=jnp.float32
    ) * HEAD ** (-0.5)
    scores = jnp.where(visible, scores, -1e30)
    shares = jnp.exp(scores - log_total[..., None])
    grad_values = jnp.einsum(
        "chqk,qche->kche",
        shares.astype(jnp.bfloat16),
        grad_mixed,
        preferred_element_type=jnp.float32,
    )
    grad_shares = jnp.einsum(
        "qche,kche->chqk", grad_mixed, values, preferred_element_type=jnp.float32
    )
    grad_scores = shares * (grad_shares - jnp.sum(shares * grad_shares, axis=-1, keepdims=True))
    low_scores = grad_scores.astype(jnp.bfloat16)
    grad_queries = jnp.einsum(
        "chqk,kche->qche", low_scores, key_rows, preferred_element_type=jnp.float32
    ) * HEAD ** (-0.5)
    grad_keys = jnp.einsum(
        "chqk,qche->kche", low_scores, queries, preferred_element_type=jnp.float32
    ) * HEAD ** (-0.5)
    return jnp.stack([grad_queries, grad_keys, grad_values], axis=2)


def branch_forward(
    hidden, norm_gain, norm_shift, input_weight, output_weight, output_bias, visible
):
    full_shape = hidden.shape
    normed = (
        norm_apply(hidden, norm_gain, norm_shift).astype(jnp.bfloat16).reshape(-1, full_shape[-1])
    )
    packed = jnp.dot(normed, input_weight, preferred_element_type=jnp.float32).astype(jnp.bfloat16)
    packed = packed.reshape(full_shape[:3] + (3, HEADS, HEAD))

    def one_block(block_items):
        return attend_block(block_items[0], block_items[1], block_items[2], block_items[3])

    mixed, log_total = lax.map(
        one_block, (packed[:, :, :, 0], packed[:, :, :, 1], packed[:, :, :, 2], visible)
    )
    mixed_flat = mixed.reshape(-1, full_shape[-1])
    branch = jnp.dot(mixed_flat, output_weight, preferred_element_type=jnp.float32) + output_bias
    return (branch.reshape(full_shape), (normed, packed, mixed_flat, log_total))


def branch_backward(
    hidden, norm_gain, norm_shift, input_weight, output_weight, visible, saved, grad_branch
):
    normed, packed, mixed_flat, log_total = saved
    full_shape = hidden.shape
    low_grad = grad_branch.astype(jnp.bfloat16)
    grad_bias = jnp.sum(low_grad.astype(jnp.float32), axis=0)
    grad_output = jnp.einsum("nd,ne->de", mixed_flat, low_grad, preferred_element_type=jnp.float32)
    grad_mixed = jnp.einsum(
        "ne,de->nd", low_grad, output_weight, preferred_element_type=jnp.float32
    )
    grad_mixed = grad_mixed.astype(jnp.bfloat16).reshape(full_shape[:3] + (HEADS, HEAD))

    def one_block(block_items):
        return attend_back(*block_items)

    grad_packed = lax.map(
        one_block,
        (
            packed[:, :, :, 0],
            packed[:, :, :, 1],
            packed[:, :, :, 2],
            visible,
            log_total,
            grad_mixed,
        ),
    )
    grad_packed = grad_packed.reshape(-1, 3 * full_shape[-1]).astype(jnp.bfloat16)
    grad_input = jnp.einsum("nd,ne->de", normed, grad_packed, preferred_element_type=jnp.float32)
    grad_normed = jnp.einsum(
        "ne,de->nd", grad_packed, input_weight, preferred_element_type=jnp.float32
    )
    token_rows = hidden.reshape(-1, full_shape[-1])
    unused, pullback = jax.vjp(norm_apply, token_rows, norm_gain, norm_shift)
    grad_rows, grad_gain, grad_shift = pullback(grad_normed)
    return (grad_rows, (grad_gain, grad_shift, grad_input, grad_output, grad_bias))


def body(
    inputs,
    context,
    sample_mask,
    sample_gain,
    sample_shift,
    sample_project,
    sample_output,
    sample_bias,
    feature_gain,
    feature_shift,
    feature_project,
    feature_output,
    feature_bias,
    dense_gain,
    dense_shift,
    up_weight,
    up_bias,
    down_weight,
    down_bias,
    cotangent,
):
    task_count, feat_count, sample_count, model_width = inputs.shape
    position = lax.broadcasted_iota(jnp.int32, (task_count, sample_count), 1)
    task_keys = (position < context[:, None]) & (sample_mask == 1)
    pair_keys = jnp.broadcast_to(task_keys[:, None, :], (task_count, feat_count, sample_count))
    pair_keys = pair_keys.reshape(-1, sample_count)
    stream_in = inputs.astype(jnp.float32).reshape(
        task_count * feat_count, sample_count, 1, model_width
    )
    sample_branch, sample_saved = branch_forward(
        stream_in, sample_gain, sample_shift, sample_project, sample_output, sample_bias, pair_keys
    )
    after_sample = (stream_in + sample_branch).reshape(inputs.shape)
    regrouped, grad_result = (
        lax.all_to_all(
            after_sample.astype(jnp.bfloat16), "feat", split_axis=2, concat_axis=1, tiled=True
        ),
        lax.all_to_all(cotangent, "feat", split_axis=2, concat_axis=1, tiled=True),
    )
    middle = regrouped.astype(jnp.float32)
    group_shape = middle.shape
    feature_keys = jnp.ones(group_shape[:2], jnp.bool_)
    feature_branch, feature_saved = branch_forward(
        middle,
        feature_gain,
        feature_shift,
        feature_project,
        feature_output,
        feature_bias,
        feature_keys,
    )
    after_feature = (middle + feature_branch).reshape(-1, model_width)
    dense_in = norm_apply(after_feature, dense_gain, dense_shift).astype(jnp.bfloat16)
    pre_act = jnp.dot(dense_in, up_weight, preferred_element_type=jnp.float32) + up_bias
    activated = jax.nn.gelu(pre_act).astype(jnp.bfloat16)
    result = (
        after_feature
        + jnp.dot(activated, down_weight, preferred_element_type=jnp.float32)
        + down_bias
    )
    output = lax.all_to_all(
        result.reshape(group_shape).astype(jnp.bfloat16),
        "feat",
        split_axis=1,
        concat_axis=2,
        tiled=True,
    )
    grad_low = grad_result.reshape(-1, model_width)
    grad_stream = grad_low.astype(jnp.float32)
    grad_down_bias = jnp.sum(grad_stream, axis=0)
    grad_down = jnp.einsum("nf,nd->fd", activated, grad_low, preferred_element_type=jnp.float32)
    grad_act = jnp.einsum("nd,fd->nf", grad_low, down_weight, preferred_element_type=jnp.float32)
    unused, gelu_pull = jax.vjp(jax.nn.gelu, pre_act)
    grad_pre = gelu_pull(grad_act)[0].astype(jnp.bfloat16)
    grad_up_bias = jnp.sum(grad_pre.astype(jnp.float32), axis=0)
    grad_up = jnp.einsum("nd,nf->df", dense_in, grad_pre, preferred_element_type=jnp.float32)
    grad_dense_in = jnp.einsum("nf,df->nd", grad_pre, up_weight, preferred_element_type=jnp.float32)
    unused_rows, norm_pull = jax.vjp(norm_apply, after_feature, dense_gain, dense_shift)
    grad_norm_rows, grad_dense_gain, grad_dense_shift = norm_pull(grad_dense_in)
    grad_after_feature = grad_stream + grad_norm_rows
    grad_feature_rows, feature_grads = branch_backward(
        middle,
        feature_gain,
        feature_shift,
        feature_project,
        feature_output,
        feature_keys,
        feature_saved,
        grad_after_feature,
    )
    (
        grad_feature_gain,
        grad_feature_shift,
        grad_feature_project,
        grad_feature_output,
        grad_feature_bias,
    ) = feature_grads
    grad_sent = (grad_after_feature + grad_feature_rows).astype(jnp.bfloat16).reshape(group_shape)
    grad_returned = lax.all_to_all(grad_sent, "feat", split_axis=1, concat_axis=2, tiled=True)
    grad_after_sample = grad_returned.astype(jnp.float32).reshape(-1, model_width)
    grad_sample_rows, sample_grads = branch_backward(
        stream_in,
        sample_gain,
        sample_shift,
        sample_project,
        sample_output,
        pair_keys,
        sample_saved,
        grad_after_sample,
    )
    (
        grad_sample_gain,
        grad_sample_shift,
        grad_sample_project,
        grad_sample_output,
        grad_sample_bias,
    ) = sample_grads
    input_grad = (grad_after_sample + grad_sample_rows).reshape(inputs.shape)
    combined = lax.psum(
        (
            grad_sample_gain,
            grad_sample_shift,
            grad_sample_project,
            grad_sample_output,
            grad_sample_bias,
            grad_feature_gain,
            grad_feature_shift,
            grad_feature_project,
            grad_feature_output,
            grad_feature_bias,
            grad_dense_gain,
            grad_dense_shift,
            grad_up,
            grad_up_bias,
            grad_down,
            grad_down_bias,
        ),
        ("task", "feat"),
    )
    return (output, input_grad) + tuple(combined)


def solution(mesh):
    return jax.shard_map(
        body,
        mesh=mesh,
        in_specs=(
            P("task", "feat", None, None),
            P("task"),
            P("task", None),
            P(),
            P(),
            P(),
            P(),
            P(),
            P(),
            P(),
            P(),
            P(),
            P(),
            P(),
            P(),
            P(),
            P(),
            P(),
            P(),
            P("task", "feat", None, None),
        ),
        out_specs=(
            P("task", "feat", None, None),
            P("task", "feat", None, None),
            P(),
            P(),
            P(),
            P(),
            P(),
            P(),
            P(),
            P(),
            P(),
            P(),
            P(),
            P(),
            P(),
            P(),
            P(),
            P(),
        ),
        check_vma=False,
    )
```

profile of v0, /device:TPU:0, one launch (start us, length us, event | category | flops | bytes accessed | tf_op | source)
XLA Modules:
  0.0 1334.4 jit_solution(14459133283832784476)
XLA Ops:
  15.4 9.7 convolution_convert_fusion.1
  25.1 16.8 %copy.147 = bf16[4096,1536]{0,1:T(8,128)(2,1)} copy(bf16[4096,1536]{1,0:T(8,128)(2,1)} %convolution_convert_fusion.1) | data formatting | bytes 25165824 | tf_op jit(solution)/shard_map/convert_element_type | solution.py:63
  41.9 9.4 copy.204
  63.2 90.0 %while.4 = (s32[]{:T(128)}, bf16[8,512,1,8,64]{1,4,3,2,0:T(8,128)(2,1)}, f32[8,1,8,512]{3,2,1,0:T(8,128)}, bf16[8,512,1,8,64]{1,4,3,2,0:T(8,128)(2,1)}, pred[8,5...) while((s32[]{:T(128)}, ...), condition=%wide.region_5.6_spmd, body=%wide.region_2.5_spmd.sunk | while | flops 562294784 | bytes 27399256 | solution.py:69
  153.2 4.8 copy.151
  164.0 5.3 add_convert_fusion.1
  169.2 4.4 copy.152
  173.6 5.7 all-to-all-start
  179.3 6.6 copy.161
  185.9 42.5 %all-to-all-done = bf16[1,8,512,512]{3,1,0,2:T(8,128)(2,1)} async-done(((bf16[1,8,512,512]{3,1,0,2:T(8,128)(2,1)}), bf16[1,8,512,512]{3,1,0,2:T(8,128)(2,1)}, u32[]{:S(2)}, u32[]{:S(2)}) %all-to-all-start) | async-done | bytes 4194336 | tf_op jit(solution)/shard_map/all_to_all | solution.py:150
  228.4 4.6 all-to-all-start.2
  236.4 4.6 bitcast_reduce_fusion
  241.0 5.5 multiply_reduce_fusion.11
  246.6 7.1 copy.153
  259.3 9.9 convolution_convert_fusion
  269.3 30.9 %reshape.577 = bf16[1,64,64,3,8,64]{5,4,3,2,1,0:T(8,128)(2,1)} reshape(bf16[4096,1536]{1,0:T(8,128)(2,1)} %convolution_convert_fusion) | data formatting | bytes 25165824 | tf_op jit(solution)/shard_map/reshape | solution.py:64
  300.2 16.8 %fusion.87 = (bf16[1,64,64,1,8,64]{5,4,3,2,1,0:T(8,128)(2,1)}, bf16[1,64,64,1,8,64]{5,4,3,2,1,0:T(8,128)(2,1)}, bf16[1,64,64,1,8,64]{5,4,3,2,1,0:T(8,128)(2,1)}) fusion(bf16[1,64,64,3,8,64]{5,4,3,2,1,0:T(8,128)(2,1)} %reshape.577), kind=kLoop, calls=%fused_computation.166 | loop fusion | bytes 25165824 | tf_op jit(solution)/shard_map/slice | solution.py:70
  317.0 12.7 copy.199
  329.7 22.7 %multiply_reduce_fusion.2 = (f32[64,8,64]{2,1,0:T(8,128)S(1)}, f32[64,8,64,64]{2,3,1,0:T(8,128)}) fusion(bf16[1,64,64,1,8,64]{5,4,3,2,1,0:T(8,128)(2,1)} %get-tuple-element.260, bf16[1,64,64,1,8,64]{5,4,3,2,1,0:T(8,128)(2,1)} %get-tuple-element.261), kind=kOutput, calls=%fused_computation.82 | convolution fusion | flops 272596992 | bytes 16908288 | tf_op jit(solution)/shard_map/while/body/eval_jaxpr/qche,kche->chqk/dot_general | solution.py:18
  352.3 11.2 fusion.57
  363.6 13.6 %convert_bitcast_fusion = bf16[64,64,8,64]{0,3,2,1:T(8,128)(2,1)} fusion(f32[64,8,64,64]{2,3,1,0:T(8,128)} %get-tuple-element.277, f32[64,8,64]{2,1,0:T(8,128)S(1)} %fusion.57, f32[64,8,64]{2,1,0:T(8,128)S(1)} %get-tuple-element.276, bf16[1,64,64,1,8,64]{1,5,4,2,3,0:T(8,128)(2,1)} %copy.199), kind=kOutput, calls=%fused_computation.121 | convolution fusion | flops 278921216 | bytes 17039360 | tf_op jit(solution)/shard_map/while/body/eval_jaxpr/chqk,kche->qche/dot_general | solution.py:26
  377.2 12.6 copy.158
  389.7 11.9 reshape.578
  401.6 7.3 fusion.88
  415.0 5.9 copy.162
  420.9 22.4 %multiply_convert_fusion.1 = (bf16[4096,2048]{1,0:T(8,128)(2,1)}, f32[4096,2048]{1,0:T(8,128)}) fusion(f32[2048]{0:T(1024)S(1)} %copy-done.69, bf16[512,2048]{1,0:T(8,128)(2,1)S(1)} %copy-done, f32[4096,512]{1,0:T(8,128)S(1)} %copy-done.7, f32[512]{0:T(512)S(1)} %copy-done.72, f32[512]{0:T(512)S(1)} %copy-done.55, f32[4096]{0:T(1024)S(1)} %fusion.74, ...), kind=kOutput, calls=%fused_computation.71 | convolution fusion | flops 8684306432 | bytes 60862464 | tf_op jit(solution)/shard_map/dot_general | solution.py:169
  443.3 34.8 %convert_reduce_fusion = (f32[2048]{0:T(1024)}, bf16[4096,2048]{1,0:T(8,128)(2,1)}) fusion(f32[4096,2048]{1,0:T(8,128)} %get-tuple-element.281, f32[2048]{0:T(1024)S(1)} %copy-done.69, bf16[4096,512]{1,0:T(8,128)(2,1)} %bitcast.296, bf16[2048,512]{1,0:T(8,128)(2,1)} %param.41), kind=kOutput, calls=%fused_computation.70 | convolution fusion | flops 8782870528 | bytes 56639488 | tf_op jit(solution)/shard_map/nd,fd->nf/dot_general | solution.py:187
  478.1 17.5 %multiply_reduce_fusion.3 = (f32[512]{0:T(512)}, f32[4096]{0:T(1024)S(1)}, f32[512]{0:T(512)}, f32[4096,512]{1,0:T(8,128)}) fusion(f32[4096,512]{1,0:T(8,128)S(1)} %copy-done.7, f32[4096]{0:T(1024)S(1)} %fusion.74, f32[4096]{0:T(1024)S(1)} %broadcast_multiply_fusion.1, f32[512]{0:T(512)S(1)} %copy-done.55, bf16[4096,2048]{1,0:T(8,128)(2,1)} %get-tuple-element.288, ...), kind=kOutput, calls=%fused_computation.103 | convolution fusion | flops 8606707712 | bytes 35706880 | tf_op jit(solution)/shard_map/nf,df->nd/dot_general | solution.py:192
  495.6 6.1 fusion.86
  507.0 4.5 convolution_convert_fusion.3
  511.5 11.2 squeeze.72
  522.8 12.8 copy.171
  535.6 19.6 %multiply_reduce_fusion.1 = (f32[64,8,64]{2,1,0:T(8,128)S(1)}, f32[64,8,64,64]{2,3,1,0:T(8,128)}) fusion(f32[64,8,64,64]{2,3,1,0:T(8,128)} %get-tuple-element.277, f32[64,8,64]{2,1,0:T(8,128)S(1)} %copy-done.18, bf16[64,64,8,64]{0,3,2,1:T(8,128)(2,1)} %copy.171, bf16[1,64,64,1,8,64]{1,5,4,2,3,0:T(8,128)(2,1)} %copy.199), kind=kOutput, calls=%fused_computation.75 | convolution fusion | flops 276791296 | bytes 25427968 | tf_op jit(solution)/shard_map/while/body/eval_jaxpr/qche,kche->chqk/dot_general | solution.py:42
  555.2 15.0 %multiply_convert_fusion.2 = bf16[64,8,64,64]{2,3,1,0:T(8,128)(2,1)} fusion(f32[64,8,64,64]{2,3,1,0:T(8,128)} %get-tuple-element.284, f32[64,8,64,64]{2,3,1,0:T(8,128)} %get-tuple-element.277, f32[64,8,64]{2,1,0:T(8,128)S(1)} %get-tuple-element.283, f32[64,8,64]{2,1,0:T(8,128)S(1)} %copy-done.18), kind=kLoop, calls=%fused_computation.74 | loop fusion | flops 10485760 | bytes 21233664 | tf_op jit(solution)/shard_map/while/body/eval_jaxpr/convert_element_type | solution.py:46
  570.1 16.3 %multiply_bitcast_fusion.1 = bf16[64,64,1,8,64]{4,0,3,1,2:T(8,128)(2,1)} fusion(bf16[64,8,64,64]{2,3,1,0:T(8,128)(2,1)} %multiply_convert_fusion.2, bf16[1,64,64,1,8,64]{5,4,3,2,1,0:T(8,128)(2,1)} %get-tuple-element.260), kind=kOutput, calls=%fused_computation.73 | convolution fusion | flops 272629760 | bytes 12582912 | tf_op jit(solution)/shard_map/while/body/eval_jaxpr/chqk,kche->qche/dot_general | solution.py:47
  586.4 18.4 %multiply_bitcast_fusion = bf16[64,64,1,8,64]{4,0,3,1,2:T(8,128)(2,1)} fusion(bf16[64,8,64,64]{2,3,1,0:T(8,128)(2,1)} %multiply_convert_fusion.2, bf16[1,64,64,1,8,64]{5,4,3,2,1,0:T(8,128)(2,1)} %get-tuple-element.261), kind=kOutput, calls=%fused_computation.72 | convolution fusion | flops 272629760 | bytes 12582912 | tf_op jit(solution)/shard_map/while/body/eval_jaxpr/chqk,qche->kche/dot_general | solution.py:50
  604.9 13.1 convolution_bitcast_fusion
  618.0 17.4 %maximum_convert_fusion = bf16[64,64,3,8,64]{4,0,3,1,2:T(8,128)(2,1)} fusion(bf16[64,64,1,8,64]{4,0,3,1,2:T(8,128)(2,1)} %convolution_bitcast_fusion, bf16[64,64,1,8,64]{4,0,3,1,2:T(8,128)(2,1)} %multiply_bitcast_fusion, bf16[64,64,1,8,64]{4,0,3,1,2:T(8,128)(2,1)} %multiply_bitcast_fusion.1), kind=kLoop, calls=%fused_computation.60 | loop fusion | flops 12582912 | bytes 25165824 | tf_op jit(solution)/shard_map/convert_element_type | solution.py:104
  635.4 25.0 %copy.174 = bf16[64,64,3,8,64]{4,3,2,1,0:T(8,128)(2,1)} copy(bf16[64,64,3,8,64]{4,0,3,1,2:T(8,128)(2,1)} %maximum_convert_fusion) | data formatting | bytes 25165824 | tf_op jit(solution)/shard_map/convert_element_type | solution.py:104
  660.4 32.6 %convert_element_type.212 = bf16[4096,1536]{1,0:T(8,128)(2,1)} reshape(bf16[64,64,3,8,64]{4,3,2,1,0:T(8,128)(2,1)} %copy.174) | data formatting | bytes 25165824 | tf_op jit(solution)/shard_map/convert_element_type | solution.py:104
  693.0 10.5 add_convert_fusion
  703.5 15.4 %multiply_reduce_fusion.4 = (f32[512]{0:T(512)}, f32[4096]{0:T(1024)S(1)}, f32[512]{0:T(512)}, f32[4096,512]{1,0:T(8,128)}) fusion(f32[1,8,8,64,512]{4,3,1,2,0:T(8,128)} %copy.153, f32[4096]{0:T(1024)S(1)} %copy-done.34, f32[4096]{0:T(1024)S(1)} %copy-done.30, f32[512]{0:T(512)S(1)} %copy-done.48, bf16[4096,1536]{1,0:T(8,128)(2,1)} %convert_element_type.212, ...), kind=kOutput, calls=%fused_computation.106 | convolution fusion | flops 6459223040 | bytes 30988288 | tf_op jit(solution)/shard_map/ne,de->nd/dot_general | solution.py:106
  719.0 8.5 fusion.85
  727.5 8.9 add_convert_fusion.2
  736.4 4.8 all-to-all-start.3
  741.2 15.1 %fusion.93 = f32[2048,512]{1,0:T(8,128)} fusion(bf16[4096,2048]{1,0:T(8,128)(2,1)} %get-tuple-element.280, bf16[4096,512]{1,0:T(8,128)(2,1)} %bitcast.297), kind=kOutput, calls=%fused_computation.172 | convolution fusion | flops 8589934592 | bytes 25165824 | tf_op jit(solution)/shard_map/nf,nd->fd/dot_general | solution.py:186
  756.3 18.0 %add_convert_fusion.3 = bf16[4096,512]{1,0:T(8,128)(2,1)} fusion(f32[4096,512]{1,0:T(8,128)} %copy-done.6, bf16[4096,2048]{1,0:T(8,128)(2,1)} %get-tuple-element.280, bf16[2048,512]{1,0:T(8,128)(2,1)S(1)} %copy-done.62, f32[512]{0:T(512)S(1)} %copy-done.71), kind=kOutput, calls=%fused_computation.118 | convolution fusion | flops 8596226048 | bytes 31459328 | tf_op jit(solution)/shard_map/dot_general | solution.py:173
  774.3 12.6 fusion.91
  790.4 17.0 %fusion.81 = f32[512,2048]{1,0:T(8,128)} fusion(bf16[4096,2048]{1,0:T(8,128)(2,1)} %get-tuple-element.288, f32[4096,512]{1,0:T(8,128)S(1)} %bitcast.292, f32[512]{0:T(512)S(1)} %copy-done.73, f32[512]{0:T(512)S(1)} %copy-done.56, f32[4096]{0:T(1024)S(1)} %copy-done.44, f32[4096]{0:T(1024)S(1)} %copy-done.32), kind=kOutput, calls=%fused_computation.161 | convolution fusion | flops 8600420352 | bytes 29396992 | tf_op jit(solution)/shard_map/nd,nf->df/dot_general | solution.py:191
  807.4 4.7 all-to-all-start.1
  821.2 11.3 reshape.586
  832.5 9.7 copy.180
  842.2 152.8 %while.5 = (s32[]{:T(128)}, bf16[8,512,1,3,8,64]{1,5,4,3,2,0:T(8,128)(2,1)}, bf16[8,512,1,8,64]{1,4,3,2,0:T(8,128)(2,1)}, pred[8,512]{1,0:T(8,128)(4,1)S(1)}, bf...) while((s32[]{:T(128)}, ...), condition=%wide.region_19.20_spmd, body=%wide.region_17.19_spmd.sunk | while | flops 1379397632 | bytes 71424608 | solution.py:93
  995.0 12.0 copy.182
  1007.0 4.7 copy.206
  1011.8 12.6 fusion.89
  1024.4 5.5 fusion.90
  1034.0 5.4 copy.160
  1039.4 12.6 fusion.83
  1052.2 5.9 convert_reduce_fusion.3
  1058.1 4.5 multiply_reduce_fusion.5
  1062.7 43.4 %all-reduce = (f32[512]{0:T(512)}, f32[512]{0:T(512)}, f32[512]{0:T(512)}, f32[512]{0:T(512)}, f32[512]{0:T(512)}, /*index=5*/f32[512]{0:T(512)}, f32[512]{0:T(512)}, f32[512]{0:T(512)}, f32[2048]{0:T(1024)}, f32[512]{0:T(512)}) all-reduce(f32[512]{0:T(512)S(1)} %get-tuple-element.197, ...), channel_id=1, replica_groups=mesh['task'=4,'feat'=8] {'task','feat'}, use_global_device_ids=true, to_apply=%region_24.25 | all-reduce | flops 6656 | bytes 53248 | tf_op jit(solution)/shard_map/psum | solution.py:234
  1106.1 10.4 add_add_fusion.3
  1116.5 197.0 %all-reduce.4.cloned.1.call-done = (f32[512,1536]{1,0:T(8,128)}, f32[512,512]{1,0:T(8,128)}, f32[512,1536]{1,0:T(8,128)}, f32[512,512]{1,0:T(8,128)}, f32[512,2048]{1,0:T(8,128)}, /*index=5*/f32[2048,512]{1,0:T(8,128)}) async-done(((f32[512,1536]{1,0:T(8,128)}, f32[512,512]{1,0:T(8,128)}, f32[512,1536]{1,0:T(8,128)}, f32[512,512]{1,0:T(8,128)}, f32[512,2048]{1,0:T(8,128)}, ...) | async-done | bytes 16777232 | tf_op jit(solution)/shard_map/psum | solution.py:234
  (323 shorter events, 306.8 us)
Async XLA Ops:
  7.2 413.7 %copy-start = (bf16[512,2048]{1,0:T(8,128)(2,1)S(1)}, bf16[512,2048]{1,0:T(8,128)(2,1)}, u32[]{:S(2)}) copy-start(bf16[512,2048]{1,0:T(8,128)(2,1)} %param.39) | copy-start | bytes 6291460
  7.2 6.5 copy-start.45
  7.2 6.5 copy-start.53
  7.2 6.4 copy-start.2
  7.3 8.1 copy-start.65
  55.6 7.5 copy-start.57
  153.2 7.0 copy-start.39
  153.2 7.1 copy-start.67
  153.2 7.1 copy-start.70
  173.6 54.8 %all-to-all-start = ((bf16[1,8,512,512]{3,1,0,2:T(8,128)(2,1)}), bf16[1,8,512,512]{3,1,0,2:T(8,128)(2,1)}, u32[]{:S(2)}, u32[]{:S(2)}) async-start(bf16[1,8,512,512]{3,1,0,2:T(8,128)(2,1)} %copy.152), calls=%async_computation | async-start | bytes 8388608 | tf_op jit(solution)/shard_map/all_to_all | solution.py:150
  228.4 186.6 %all-to-all-start.2 = ((bf16[1,8,512,512]{3,1,0,2:T(8,128)(2,1)}), bf16[1,8,512,512]{3,1,0,2:T(8,128)(2,1)}, u32[]{:S(2)}, u32[]{:S(2)}) async-start(bf16[1,8,512,512]{3,1,0,2:T(8,128)(2,1)} %copy.161), calls=%async_computation.2 | async-start | bytes 8388608 | tf_op jit(solution)/shard_map/all_to_all | solution.py:153
  241.0 12.8 copy-start.25
  246.5 8.6 copy-start.47
  246.5 8.5 copy-start.49
  246.6 12.7 copy-start.29
  254.5 14.8 %copy-start.37 = (f32[4096]{0:T(1024)}, f32[4096]{0:T(1024)S(1)}, u32[]{:S(2)}) copy-start(f32[4096]{0:T(1024)S(1)} %add.238) | copy-start | bytes 49156
  389.7 11.9 copy-start.24
  389.7 11.9 copy-start.54
  409.0 86.7 %copy-start.31 = (f32[4096]{0:T(1024)}, f32[4096]{0:T(1024)S(1)}, u32[]{:S(2)}) copy-start(f32[4096]{0:T(1024)S(1)} %broadcast_multiply_fusion.1) | copy-start | bytes 49156
  412.2 8.7 copy-start.55
  412.2 8.7 copy-start.69
  412.2 8.7 copy-start.72
  414.2 81.4 %copy-start.43 = (f32[4096]{0:T(1024)}, f32[4096]{0:T(1024)S(1)}, u32[]{:S(2)}) copy-start(f32[4096]{0:T(1024)S(1)} %fusion.74) | copy-start | bytes 49156
  415.0 5.9 copy-start.7
  495.6 6.1 copy-start.10
  522.8 12.8 copy-start.18
  660.4 32.6 %copy-start.26 = (f32[8,8,64]{2,1,0:T(8,128)S(1)}, f32[8,8,64]{2,1,0:T(8,128)}, u32[]{:S(2)}) copy-start(f32[8,8,64]{2,1,0:T(8,128)} %copy-done.25) | copy-start | bytes 49156
  660.4 32.6 %copy-start.41 = (f32[8,8,64]{2,1,0:T(8,128)S(1)}, f32[8,8,64]{2,1,0:T(8,128)}, u32[]{:S(2)}) copy-start(f32[8,8,64]{2,1,0:T(8,128)} %get-tuple-element.268) | copy-start | bytes 49156
  660.4 32.6 %copy-start.48 = (f32[512]{0:T(512)S(1)}, f32[512]{0:T(512)}, u32[]{:S(2)}) copy-start(f32[512]{0:T(512)} %param.32) | copy-start | bytes 6148
  660.4 32.6 %copy-start.50 = (f32[512]{0:T(512)S(1)}, f32[512]{0:T(512)}, u32[]{:S(2)}) copy-start(f32[512]{0:T(512)} %param.33) | copy-start | bytes 6148
  693.0 10.5 copy-start.30
  693.0 10.5 copy-start.34
  693.0 10.5 copy-start.64
  693.0 26.0 %slice-start = ((s8[8388608]{0:T(1024)(128)(4,1)}), s8[4194304]{0:T(1024)(128)(4,1)S(1)}, s32[]{:S(2)}) async-start(s8[8388608]{0:T(1024)(128)(4,1)} %bitcast.289), calls=%async_computation.5 | async-start | bytes 8388608
  703.5 15.5 %copy-start.38 = (f32[4096]{0:T(1024)S(1)}, f32[4096]{0:T(1024)}, u32[]{:S(2)}) copy-start(f32[4096]{0:T(1024)} %copy-done.37) | copy-start | bytes 49156
  703.5 15.5 %slice-start.1 = ((s8[8388608]{0:T(1024)(128)(4,1)}), s8[4194304]{0:T(1024)(128)(4,1)S(1)}, s32[]{:S(2)}) async-start(s8[8388608]{0:T(1024)(128)(4,1)} %bitcast.289), calls=%async_computation.6 | async-start | bytes 8388608
  719.0 8.5 copy-start.11
  719.0 8.5 copy-start.36
  736.4 71.0 %all-to-all-start.3 = ((bf16[1,64,64,512]{3,2,0,1:T(8,128)(2,1)}), bf16[1,64,64,512]{3,2,0,1:T(8,128)(2,1)}, u32[]{:S(2)}, u32[]{:S(2)}) async-start(bf16[1,64,64,512]{3,2,0,1:T(8,128)(2,1)} %bitcast.301), calls=%async_computation.3 | async-start | bytes 8388608 | tf_op jit(solution)/shard_map/all_to_all | solution.py:214
  741.2 15.1 %copy-start.62 = (bf16[2048,512]{1,0:T(8,128)(2,1)S(1)}, bf16[2048,512]{1,0:T(8,128)(2,1)}, u32[]{:S(2)}) copy-start(bf16[2048,512]{1,0:T(8,128)(2,1)} %param.41) | copy-start | bytes 6291460
  741.2 15.1 %copy-start.71 = (f32[512]{0:T(512)S(1)}, f32[512]{0:T(512)}, u32[]{:S(2)}) copy-start(f32[512]{0:T(512)} %param.42) | copy-start | bytes 6148
  741.2 49.2 %slice-start.2 = ((s8[8388608]{0:T(1024)(128)(4,1)}), s8[4194304]{0:T(1024)(128)(4,1)S(1)}, s32[]{:S(2)}) async-start(s8[8388608]{0:T(1024)(128)(4,1)} %bitcast.291), calls=%async_computation.7 | async-start | bytes 8388608
  756.3 34.1 %slice-start.3 = ((s8[8388608]{0:T(1024)(128)(4,1)}), s8[4194304]{0:T(1024)(128)(4,1)S(1)}, s32[]{:S(2)}) async-start(s8[8388608]{0:T(1024)(128)(4,1)} %bitcast.291), calls=%async_computation.8 | async-start | bytes 8388608
  774.3 12.7 copy-start.8
  774.3 12.7 copy-start.14
  807.4 9.5 copy-start.68
  807.4 226.7 %all-to-all-start.1 = ((bf16[1,64,64,512]{3,2,0,1:T(8,128)(2,1)}), bf16[1,64,64,512]{3,2,0,1:T(8,128)(2,1)}, u32[]{:S(2)}, u32[]{:S(2)}) async-start(bf16[1,64,64,512]{3,2,0,1:T(8,128)(2,1)} %bitcast.308), calls=%async_computation.1 | async-start | bytes 8388608 | tf_op jit(solution)/shard_map/all_to_all | solution.py:176
  812.1 501.4 %all-reduce.4.cloned.1.call-start = ((), (), s32[]{:S(2)}) async-start(), calls=%async_computation.4 | async-start | bytes 33554432 | tf_op jit(solution)/shard_map/psum | solution.py:234
  832.5 9.7 copy-start.40
  1011.8 12.6 copy-start.17
  1011.8 12.6 copy-start.16
  1030.0 9.5 copy-start.28
  1030.0 9.5 copy-start.46
  1030.0 9.4 copy-start.66
  1052.1 10.5 copy-start.12
  1052.1 10.5 copy-start.51
  1052.1 10.5 copy-start.52
  1052.1 10.5 copy-start.58
  1052.2 10.5 copy-start.59
  1052.2 10.5 copy-start.60
  1052.2 10.5 copy-start.61
  1313.5 6.8 copy-start.22
  1313.5 8.5 copy-start.23
  1313.5 9.4 copy-start.21
  (19 other events, 62.9 us)
Sparse Core Ops, SparseCore 0:
  1030.1 283.3 all-reduce.3
where the time goes:
time: 1350 us; the launch traced here: 1330 us
  matrix products  499 us (37%)
  local copies, waits for them, and re-layouts  311 us (23%)
  waiting for transfers between devices  240 us (18%)
  other arithmetic  193 us (14%)
  blocking collectives  43.4 us (3%)
  starting transfers between devices  19.8 us (1%)
  between operations  16.2 us (1%)
    psum x1, waiting for transfers between devices, body(): lax.psum((grad_sample_gain, grad_sample_shift, grad_sample_project, grad_...  197 us
    convert_element_type x3, local copies, waits for them, and re-layouts, branch_backward(): grad_packed.reshape(-1, 3 * full_shape[-1]).astype(jnp.bfloat16)  69.5 us
    unnamed x170, local copies, waits for them, and re-layouts  59.8 us
    dot_general x9, matrix products, attend_back(): jnp.einsum('qche,kche->chqk', grad_mixed, values, preferred_element_type=...  52.1 us
    dot_general x9, matrix products, attend_block(): jnp.einsum('qche,kche->chqk', queries, key_rows, preferred_element_type=j...  47.7 us
    dot_general x9, matrix products, attend_block(): jnp.einsum('chqk,kche->qche', shares, values, preferred_element_type=jnp....  46 us
    psum x1, blocking collectives, body(): lax.psum((grad_sample_gain, grad_sample_shift, grad_sample_project, grad_...  43.4 us
    all_to_all x1, waiting for transfers between devices, body(): lax.all_to_all(after_sample.astype(jnp.bfloat16), 'feat', split_axis=2, c...  42.5 us
  transfers between devices with their start and end apart: 5, of which 2 were waited for; matrix products, arithmetic and copies ran while one was open for 38% of the time, Pallas kernels for 0%

commit v1 on v0

--- a/solution.py
+++ b/solution.py
@@ -146,10 +146,27 @@
         stream_in, sample_gain, sample_shift, sample_project, sample_output, sample_bias, pair_keys
     )
     after_sample = (stream_in + sample_branch).reshape(inputs.shape)
+
+    def fill_the_run(t0, across):
+        long_array, row_out = (lax.axis_size(across), lax.axis_index(across))
+        current_block = t0.shape[2] // long_array
+        a_now = jnp.roll(t0, -row_out * current_block, axis=2)
+        store = [lax.slice_in_dim(a_now, 0, current_block, axis=2)]
+        k = 1
+        while k < long_array:
+            local_out = lax.slice_in_dim(a_now, k * current_block, (k + 1) * current_block, axis=2)
+            store.append(
+                lax.ppermute(
+                    local_out, across, [(w, (w + k) % long_array) for w in range(long_array)]
+                )
+            )
+            k += 1
+        return jnp.roll(
+            jnp.concatenate(store[::-1], axis=1), (row_out + 1) * store[0].shape[1], axis=1
+        )
+
     regrouped, grad_result = (
-        lax.all_to_all(
-            after_sample.astype(jnp.bfloat16), "feat", split_axis=2, concat_axis=1, tiled=True
-        ),
+        fill_the_run(after_sample.astype(jnp.bfloat16), "feat"),
         lax.all_to_all(cotangent, "feat", split_axis=2, concat_axis=1, tiled=True),
     )
     middle = regrouped.astype(jnp.float32)

time: 1350 us -> 1380 us (1.022)
  waiting for transfers between devices: 240 us -> 296 us
    ppermute x0 -> x7, waiting for transfers between devices: none -> 75.6 us  [fill_the_run(): lax.ppermute(local_out, across, [(w, (w + k) % long_array) for w in range...]
    all_to_all x1 -> x0, waiting for transfers between devices: 42.5 us -> none  [body(): lax.all_to_all(after_sample.astype(jnp.bfloat16), 'feat', split_axis=2, c...]
    all_to_all x1, waiting for transfers between devices: 0.01 us -> 22.9 us  [body(): lax.all_to_all(grad_sent, 'feat', split_axis=1, concat_axis=2, tiled=True)]
    unnamed x170 -> x165, local copies, waits for them, and re-layouts: 59.8 us -> 69.1 us
  transfers between devices with their start and end apart: 5 -> 11, of which waited for: 2 -> 7; matrix products, arithmetic and copies ran while one was open for 38% -> 37% of each run, Pallas kernels for 0% -> 0%
where the time goes in v1:
time: 1380 us; the launch traced here: 1370 us
  matrix products  493 us (36%)
  local copies, waits for them, and re-layouts  313 us (23%)
  waiting for transfers between devices  296 us (21%)
  other arithmetic  183 us (13%)
  blocking collectives  42.9 us (3%)
  starting transfers between devices  21.6 us (2%)
  between operations  16.2 us (1%)
    psum x1, waiting for transfers between devices, body(): lax.psum((grad_sample_gain, grad_sample_shift, grad_sample_project, grad_...  197 us
    ppermute x7, waiting for transfers between devices, fill_the_run(): lax.ppermute(local_out, across, [(w, (w + k) % long_array) for w in range...  75.6 us
    convert_element_type x3, local copies, waits for them, and re-layouts, branch_backward(): grad_packed.reshape(-1, 3 * full_shape[-1]).astype(jnp.bfloat16)  69.6 us
    unnamed x165, local copies, waits for them, and re-layouts  69.1 us
    dot_general x9, matrix products, attend_back(): jnp.einsum('qche,kche->chqk', grad_mixed, values, preferred_element_type=...  51.9 us
    dot_general x9, matrix products, attend_block(): jnp.einsum('qche,kche->chqk', queries, key_rows, preferred_element_type=j...  48.2 us
    dot_general x9, matrix products, attend_block(): jnp.einsum('chqk,kche->qche', shares, values, preferred_element_type=jnp....  46.1 us
    psum x1, blocking collectives, body(): lax.psum((grad_sample_gain, grad_sample_shift, grad_sample_project, grad_...  42.9 us
  transfers between devices with their start and end apart: 11, of which 7 were waited for; matrix products, arithmetic and copies ran while one was open for 37% of the time, Pallas kernels for 0%

profile of v1, /device:TPU:0, one launch (start us, length us, event | category | flops | bytes accessed | tf_op | source)
XLA Modules:
  0.0 1365.8 jit_solution(16253785950127791128)
XLA Ops:
  15.4 9.7 convolution_convert_fusion.1
  25.1 16.8 %copy.103 = bf16[4096,1536]{0,1:T(8,128)(2,1)} copy(bf16[4096,1536]{1,0:T(8,128)(2,1)} %convolution_convert_fusion.1) | data formatting | bytes 25165824 | tf_op jit(solution)/shard_map/convert_element_type | solution.py:63
  41.9 9.4 copy.158
  63.1 79.0 %while.4 = (s32[]{:T(128)}, bf16[8,512,1,8,64]{1,4,3,2,0:T(8,128)(2,1)}, f32[8,1,8,512]{3,2,1,0:T(8,128)}, bf16[8,512,1,8,64]{1,4,3,2,0:T(8,128)(2,1)}, pred[8,5...) while((s32[]{:T(128)}, ...), condition=%wide.region_5.6_spmd, body=%wide.region_2.5_spmd.sunk | while | flops 562294784 | bytes 27399256 | solution.py:69
  142.1 4.8 copy.107
  151.2 4.8 convolution_add_fusion.1
  156.0 5.4 add_convert_fusion
  174.3 4.4 copy.115
  178.7 4.6 all-to-all-start.1
  185.7 9.7 collective-permute-done.1
  200.0 6.7 collective-permute-done.4
  207.7 56.0 %collective-permute-done.5 = bf16[1,8,64,512]{3,2,1,0:T(8,128)(2,1)S(1)} collective-permute-done((bf16[1,8,64,512]{3,2,1,0:T(8,128)(2,1)}, bf16[1,8,64,512]{3,2,1,0:T(8,128)(2,1)S(1)}, u32[]{:S(2)}, u32[]{:S(2)}) %collective-permute-start.5) | collective-permute-done | bytes 524320 | tf_op jit(solution)/shard_map/ppermute | solution.py:159
  276.8 9.8 convolution_convert_fusion
  286.5 30.9 %reshape.546 = bf16[1,64,64,3,8,64]{5,4,3,2,1,0:T(8,128)(2,1)} reshape(bf16[4096,1536]{1,0:T(8,128)(2,1)} %convolution_convert_fusion) | data formatting | bytes 25165824 | tf_op jit(solution)/shard_map/reshape | solution.py:64
  317.5 16.8 %fusion.89 = (bf16[1,64,64,1,8,64]{5,4,3,2,1,0:T(8,128)(2,1)}, bf16[1,64,64,1,8,64]{5,4,3,2,1,0:T(8,128)(2,1)}, bf16[1,64,64,1,8,64]{5,4,3,2,1,0:T(8,128)(2,1)}) fusion(bf16[1,64,64,3,8,64]{5,4,3,2,1,0:T(8,128)(2,1)} %reshape.546), kind=kLoop, calls=%fused_computation.186 | loop fusion | bytes 25165824 | tf_op jit(solution)/shard_map/slice | solution.py:70
  334.3 12.7 copy.153
  346.9 23.1 %multiply_reduce_fusion.2 = (f32[64,8,64]{2,1,0:T(8,128)S(1)}, f32[64,8,64,64]{2,3,1,0:T(8,128)}) fusion(bf16[1,64,64,1,8,64]{5,4,3,2,1,0:T(8,128)(2,1)} %get-tuple-element.246, bf16[1,64,64,1,8,64]{5,4,3,2,1,0:T(8,128)(2,1)} %get-tuple-element.247), kind=kOutput, calls=%fused_computation.82 | convolution fusion | flops 272596992 | bytes 16908288 | tf_op jit(solution)/shard_map/while/body/eval_jaxpr/qche,kche->chqk/dot_general | solution.py:18
  370.0 11.2 fusion.57
  381.2 13.6 convert_bitcast_fusion
  394.9 12.5 copy.112
  407.4 12.0 reshape.547
  419.4 4.5 convolution_add_fusion
  424.0 6.4 fusion.88
  441.4 22.3 %multiply_convert_fusion.1 = (bf16[4096,2048]{1,0:T(8,128)(2,1)}, f32[4096,2048]{1,0:T(8,128)}) fusion(f32[2048]{0:T(1024)S(1)} %copy-done.62, bf16[4096,512]{1,0:T(8,128)(2,1)S(1)} %add_convert_fusion.2, bf16[512,2048]{1,0:T(8,128)(2,1)S(1)} %copy-done), kind=kOutput, calls=%fused_computation.71 | convolution fusion | flops 8673820672 | bytes 56631296 | tf_op jit(solution)/shard_map/dot_general | solution.py:186
  465.8 18.4 %fusion.61 = bf16[4096,512]{1,0:T(8,128)(2,1)} fusion(f32[1,64,64,512]{3,2,1,0:T(8,128)} %get-tuple-element.240, bf16[4096,2048]{1,0:T(8,128)(2,1)} %get-tuple-element.273, bf16[2048,512]{1,0:T(8,128)(2,1)} %param.41, f32[512]{0:T(512)S(1)} %copy-done.65), kind=kOutput, calls=%fused_computation.96 | convolution fusion | flops 8596226048 | bytes 31459328 | tf_op jit(solution)/shard_map/dot_general | solution.py:190
  484.2 5.9 copy.116
  490.1 34.5 %convert_reduce_fusion = (f32[2048]{0:T(1024)}, bf16[4096,2048]{1,0:T(8,128)(2,1)}) fusion(f32[4096,2048]{1,0:T(8,128)} %get-tuple-element.274, f32[2048]{0:T(1024)S(1)} %copy-done.62, bf16[4096,512]{1,0:T(8,128)(2,1)} %bitcast.303, bf16[2048,512]{1,0:T(8,128)(2,1)S(1)} %copy-done.53), kind=kOutput, calls=%fused_computation.70 | convolution fusion | flops 8782870528 | bytes 56639488 | tf_op jit(solution)/shard_map/nd,fd->nf/dot_general | solution.py:204
  524.6 15.4 %fusion.95 = f32[512,2048]{1,0:T(8,128)} fusion(bf16[4096,512]{1,0:T(8,128)(2,1)} %copy-done.21, bf16[4096,2048]{1,0:T(8,128)(2,1)} %get-tuple-element.281), kind=kOutput, calls=%fused_computation.192 | convolution fusion | flops 8589934592 | bytes 25165824 | tf_op jit(solution)/shard_map/nd,nf->df/dot_general | solution.py:208
  540.0 17.1 %multiply_reduce_fusion.3 = (f32[512]{0:T(512)}, f32[4096]{0:T(1024)S(1)}, f32[512]{0:T(512)}, f32[4096,512]{1,0:T(8,128)}) fusion(f32[1,64,64,512]{3,2,1,0:T(8,128)S(1)} %bitcast.299, f32[4096]{0:T(1024)S(1)} %rsqrt.54, f32[4096]{0:T(1024)S(1)} %div.97, f32[512]{0:T(512)S(1)} %copy-done.42, bf16[4096,2048]{1,0:T(8,128)(2,1)} %get-tuple-element.281, ...), kind=kOutput, calls=%fused_computation.106 | convolution fusion | flops 8606707712 | bytes 35706880 | tf_op jit(solution)/shard_map/nf,df->nd/dot_general | solution.py:209
  557.2 6.3 fusion.87
  572.0 4.6 convolution_convert_fusion.3
  576.6 11.2 squeeze.72
  587.8 12.8 copy.125
  600.6 19.4 %multiply_reduce_fusion.1 = (f32[64,8,64]{2,1,0:T(8,128)S(1)}, f32[64,8,64,64]{2,3,1,0:T(8,128)}) fusion(f32[64,8,64,64]{2,3,1,0:T(8,128)} %get-tuple-element.272, f32[64,8,64]{2,1,0:T(8,128)S(1)} %copy-done.16, bf16[64,64,8,64]{0,3,2,1:T(8,128)(2,1)} %copy.125, bf16[1,64,64,1,8,64]{1,5,4,2,3,0:T(8,128)(2,1)} %copy.153), kind=kOutput, calls=%fused_computation.75 | convolution fusion | flops 276791296 | bytes 25427968 | tf_op jit(solution)/shard_map/while/body/eval_jaxpr/qche,kche->chqk/dot_general | solution.py:42
  620.0 14.9 %multiply_convert_fusion.2 = bf16[64,8,64,64]{2,3,1,0:T(8,128)(2,1)} fusion(f32[64,8,64,64]{2,3,1,0:T(8,128)} %get-tuple-element.277, f32[64,8,64,64]{2,3,1,0:T(8,128)} %get-tuple-element.272, f32[64,8,64]{2,1,0:T(8,128)S(1)} %get-tuple-element.276, f32[64,8,64]{2,1,0:T(8,128)S(1)} %copy-done.16), kind=kLoop, calls=%fused_computation.74 | loop fusion | flops 10485760 | bytes 21233664 | tf_op jit(solution)/shard_map/while/body/eval_jaxpr/convert_element_type | solution.py:46
  634.9 16.1 %multiply_bitcast_fusion.1 = bf16[64,64,1,8,64]{4,0,3,1,2:T(8,128)(2,1)} fusion(bf16[64,8,64,64]{2,3,1,0:T(8,128)(2,1)} %multiply_convert_fusion.2, bf16[1,64,64,1,8,64]{5,4,3,2,1,0:T(8,128)(2,1)} %get-tuple-element.246), kind=kOutput, calls=%fused_computation.73 | convolution fusion | flops 272629760 | bytes 12582912 | tf_op jit(solution)/shard_map/while/body/eval_jaxpr/chqk,kche->qche/dot_general | solution.py:47
  651.0 18.4 %multiply_bitcast_fusion = bf16[64,64,1,8,64]{4,0,3,1,2:T(8,128)(2,1)} fusion(bf16[64,8,64,64]{2,3,1,0:T(8,128)(2,1)} %multiply_convert_fusion.2, bf16[1,64,64,1,8,64]{5,4,3,2,1,0:T(8,128)(2,1)} %get-tuple-element.247), kind=kOutput, calls=%fused_computation.72 | convolution fusion | flops 272629760 | bytes 12582912 | tf_op jit(solution)/shard_map/while/body/eval_jaxpr/chqk,qche->kche/dot_general | solution.py:50
  669.4 13.5 convolution_bitcast_fusion
  682.9 17.4 %maximum_convert_fusion = bf16[64,64,3,8,64]{4,0,3,1,2:T(8,128)(2,1)} fusion(bf16[64,64,1,8,64]{4,0,3,1,2:T(8,128)(2,1)} %convolution_bitcast_fusion, bf16[64,64,1,8,64]{4,0,3,1,2:T(8,128)(2,1)} %multiply_bitcast_fusion, bf16[64,64,1,8,64]{4,0,3,1,2:T(8,128)(2,1)} %multiply_bitcast_fusion.1), kind=kLoop, calls=%fused_computation.60 | loop fusion | flops 12582912 | bytes 25165824 | tf_op jit(solution)/shard_map/convert_element_type | solution.py:104
  700.4 25.0 %copy.128 = bf16[64,64,3,8,64]{4,3,2,1,0:T(8,128)(2,1)} copy(bf16[64,64,3,8,64]{4,0,3,1,2:T(8,128)(2,1)} %maximum_convert_fusion) | data formatting | bytes 25165824 | tf_op jit(solution)/shard_map/convert_element_type | solution.py:104
  725.4 32.6 %convert_element_type.174 = bf16[4096,1536]{1,0:T(8,128)(2,1)} reshape(bf16[64,64,3,8,64]{4,3,2,1,0:T(8,128)(2,1)} %copy.128) | data formatting | bytes 25165824 | tf_op jit(solution)/shard_map/convert_element_type | solution.py:104
  758.0 12.6 fusion.84
  770.7 6.4 multiply_reduce_fusion.4
  777.0 8.5 add_convert_fusion.1
  785.6 4.7 all-to-all-start.2
  790.3 12.3 fusion.93
  802.6 13.9 %fusion.96 = f32[2048,512]{1,0:T(8,128)} fusion(bf16[4096,2048]{1,0:T(8,128)(2,1)} %get-tuple-element.273, bf16[4096,512]{1,0:T(8,128)(2,1)S(1)} %bitcast.304), kind=kOutput, calls=%fused_computation.193 | convolution fusion | flops 8589934592 | bytes 25165824 | tf_op jit(solution)/shard_map/nf,nd->fd/dot_general | solution.py:203
  816.5 22.9 %all-to-all-done.2 = bf16[1,64,64,512]{3,2,0,1:T(8,128)(2,1)} async-done(((bf16[1,64,64,512]{3,2,0,1:T(8,128)(2,1)}), bf16[1,64,64,512]{3,2,0,1:T(8,128)(2,1)}, u32[]{:S(2)}, u32[]{:S(2)}) %all-to-all-start.2) | async-done | bytes 4194336 | tf_op jit(solution)/shard_map/all_to_all | solution.py:231
  839.4 4.7 all-to-all-start
  848.8 4.4 convolution_convert_fusion.2
  853.2 11.3 reshape.555
  864.5 9.8 copy.134
  874.3 152.8 %while.5 = (s32[]{:T(128)}, bf16[8,512,1,3,8,64]{1,5,4,3,2,0:T(8,128)(2,1)}, bf16[8,512,1,8,64]{1,4,3,2,0:T(8,128)(2,1)}, pred[8,512]{1,0:T(8,128)(4,1)S(1)}, bf...) while((s32[]{:T(128)}, ...), condition=%wide.region_19.20_spmd, body=%wide.region_17.19_spmd.sunk | while | flops 1379397632 | bytes 71424608 | solution.py:93
  1027.0 12.0 copy.136
  1039.1 4.7 copy.160
  1043.8 12.8 fusion.91
  1056.7 5.5 fusion.92
  1066.3 5.1 copy.114
  1071.4 12.6 fusion.85
  1084.1 5.9 convert_reduce_fusion.3
  1090.0 4.5 multiply_reduce_fusion.5
  1094.6 42.9 %all-reduce = (f32[512]{0:T(512)}, f32[512]{0:T(512)}, f32[512]{0:T(512)}, f32[512]{0:T(512)}, f32[512]{0:T(512)}, /*index=5*/f32[512]{0:T(512)}, f32[512]{0:T(512)}, f32[512]{0:T(512)}, f32[2048]{0:T(1024)}, f32[512]{0:T(512)}) all-reduce(f32[512]{0:T(512)S(1)} %get-tuple-element.182, ...), channel_id=1, replica_groups=mesh['task'=4,'feat'=8] {'task','feat'}, use_global_device_ids=true, to_apply=%region_24.25 | all-reduce | flops 6656 | bytes 53248 | tf_op jit(solution)/shard_map/psum | solution.py:251
  1137.5 10.4 add_add_fusion.3
  1147.9 197.0 %all-reduce.4.cloned.1.call-done = (f32[512,1536]{1,0:T(8,128)}, f32[512,512]{1,0:T(8,128)}, f32[512,1536]{1,0:T(8,128)}, f32[512,512]{1,0:T(8,128)}, f32[512,2048]{1,0:T(8,128)}, /*index=5*/f32[2048,512]{1,0:T(8,128)}) async-done(((f32[512,1536]{1,0:T(8,128)}, f32[512,512]{1,0:T(8,128)}, f32[512,1536]{1,0:T(8,128)}, f32[512,512]{1,0:T(8,128)}, f32[512,2048]{1,0:T(8,128)}, ...) | async-done | bytes 16777232 | tf_op jit(solution)/shard_map/psum | solution.py:251
  (332 shorter events, 332.3 us)
Async XLA Ops:
  7.2 434.2 %copy-start = (bf16[512,2048]{1,0:T(8,128)(2,1)S(1)}, bf16[512,2048]{1,0:T(8,128)(2,1)}, u32[]{:S(2)}) copy-start(bf16[512,2048]{1,0:T(8,128)(2,1)} %param.39) | copy-start | bytes 6291460
  7.2 6.5 copy-start.38
  7.2 6.5 copy-start.46
  7.3 6.4 copy-start.2
  7.3 8.1 copy-start.56
  55.6 7.5 copy-start.48
  142.1 9.0 copy-start.33
  142.1 9.0 copy-start.60
  142.1 9.0 copy-start.63
  161.4 12.9 copy-start.17
  168.3 15.9 %collective-permute-start = (bf16[1,8,64,512]{3,2,1,0:T(8,128)(2,1)}, bf16[1,8,64,512]{3,2,1,0:T(8,128)(2,1)S(1)}, u32[]{:S(2)}, u32[]{:S(2)}) collective-permute-start(bf16[1,8,64,512]{3,2,1,0:T(8,128)(2,1)} %get-tuple-element.260), channel_id=1, source_target_pairs={{0,7},{1,0},{2,1},{3,2},{4,3},{5,4},{6,5},{7,6},{8,15},{9,8},{10,9... | collective-permute-start | bytes 1572872 | tf_op jit(solution)/shard_map/ppermute | solution.py:159
  171.6 23.8 %collective-permute-start.1 = (bf16[1,8,64,512]{3,2,1,0:T(8,128)(2,1)}, bf16[1,8,64,512]{3,2,1,0:T(8,128)(2,1)S(1)}, u32[]{:S(2)}, u32[]{:S(2)}) collective-permute-start(bf16[1,8,64,512]{3,2,1,0:T(8,128)(2,1)} %get-tuple-element.259), channel_id=1, source_target_pairs={{0,6},{1,7},{2,0},{3,1},{4,2},{5,3},{6,4},{7,5},{8,14},{9,15},{10,... | collective-permute-start | bytes 1572872 | tf_op jit(solution)/shard_map/ppermute | solution.py:159
  172.2 23.3 %collective-permute-start.2 = (bf16[1,8,64,512]{3,2,1,0:T(8,128)(2,1)}, bf16[1,8,64,512]{3,2,1,0:T(8,128)(2,1)}, u32[]{:S(2)}, u32[]{:S(2)}) collective-permute-start(bf16[1,8,64,512]{3,2,1,0:T(8,128)(2,1)} %get-tuple-element.258), channel_id=1, source_target_pairs={{0,5},{1,6},{2,7},{3,0},{4,1},{5,2},{6,3},{7,4},{8,13},{9,14},{10,... | collective-permute-start | bytes 1572872 | tf_op jit(solution)/shard_map/ppermute | solution.py:159
  172.5 26.3 %collective-permute-start.3 = (bf16[1,8,64,512]{3,2,1,0:T(8,128)(2,1)}, bf16[1,8,64,512]{3,2,1,0:T(8,128)(2,1)}, u32[]{:S(2)}, u32[]{:S(2)}) collective-permute-start(bf16[1,8,64,512]{3,2,1,0:T(8,128)(2,1)} %get-tuple-element.257), channel_id=1, source_target_pairs={{0,4},{1,5},{2,6},{3,7},{4,0},{5,1},{6,2},{7,3},{8,12},{9,13},{10,... | collective-permute-start | bytes 1572872 | tf_op jit(solution)/shard_map/ppermute | solution.py:159
  174.1 32.6 %collective-permute-start.4 = (bf16[1,8,64,512]{3,2,1,0:T(8,128)(2,1)}, bf16[1,8,64,512]{3,2,1,0:T(8,128)(2,1)}, u32[]{:S(2)}, u32[]{:S(2)}) collective-permute-start(bf16[1,8,64,512]{3,2,1,0:T(8,128)(2,1)} %get-tuple-element.256), channel_id=1, source_target_pairs={{0,3},{1,4},{2,5},{3,6},{4,7},{5,0},{6,1},{7,2},{8,11},{9,12},{10,... | collective-permute-start | bytes 1572872 | tf_op jit(solution)/shard_map/ppermute | solution.py:159
  178.7 305.5 %all-to-all-start.1 = ((bf16[1,8,512,512]{3,1,0,2:T(8,128)(2,1)}), bf16[1,8,512,512]{3,1,0,2:T(8,128)(2,1)}, u32[]{:S(2)}, u32[]{:S(2)}) async-start(bf16[1,8,512,512]{3,1,0,2:T(8,128)(2,1)} %copy.115), calls=%async_computation.1 | async-start | bytes 8388608 | tf_op jit(solution)/shard_map/all_to_all | solution.py:170
  184.2 79.6 %collective-permute-start.5 = (bf16[1,8,64,512]{3,2,1,0:T(8,128)(2,1)}, bf16[1,8,64,512]{3,2,1,0:T(8,128)(2,1)S(1)}, u32[]{:S(2)}, u32[]{:S(2)}) collective-permute-start(bf16[1,8,64,512]{3,2,1,0:T(8,128)(2,1)} %get-tuple-element.255), channel_id=1, source_target_pairs={{0,2},{1,3},{2,4},{3,5},{4,6},{5,7},{6,0},{7,1},{8,10},{9,11},{10,... | collective-permute-start | bytes 1572872 | tf_op jit(solution)/shard_map/ppermute | solution.py:159
  195.5 68.4 %collective-permute-start.6 = (bf16[1,8,64,512]{3,2,1,0:T(8,128)(2,1)}, bf16[1,8,64,512]{3,2,1,0:T(8,128)(2,1)S(1)}, u32[]{:S(2)}, u32[]{:S(2)}) collective-permute-start(bf16[1,8,64,512]{3,2,1,0:T(8,128)(2,1)} %get-tuple-element.254), channel_id=1, source_target_pairs={{0,1},{1,2},{2,3},{3,4},{4,5},{5,6},{6,7},{7,0},{8,9},{9,10},{10,1... | collective-permute-start | bytes 1572872 | tf_op jit(solution)/shard_map/ppermute | solution.py:159
  265.0 7.9 copy-start.40
  265.0 7.9 copy-start.52
  269.5 5.3 copy-start.5
  269.5 7.3 copy-start.54
  407.4 12.0 copy-start.58
  407.4 12.0 copy-start.64
  434.6 6.8 copy-start.62
  441.4 22.3 %copy-start.25 = (f32[64,64]{1,0:T(8,128)S(1)}, f32[64,64]{1,0:T(8,128)}, u32[]{:S(2)}) copy-start(f32[64,64]{1,0:T(8,128)} %copy-done.24) | copy-start | bytes 49156
  441.4 23.0 %copy-start.35 = (f32[64,64]{1,0:T(8,128)S(1)}, f32[64,64]{1,0:T(8,128)}, u32[]{:S(2)}) copy-start(f32[64,64]{1,0:T(8,128)} %get-tuple-element.261) | copy-start | bytes 49156
  441.4 24.4 %copy-start.65 = (f32[512]{0:T(512)S(1)}, f32[512]{0:T(512)}, u32[]{:S(2)}) copy-start(f32[512]{0:T(512)} %param.42) | copy-start | bytes 6148
  484.2 5.9 copy-start.53
  484.2 55.8 %slice-start = ((s8[8388608]{0:T(1024)(128)(4,1)}), s8[4194304]{0:T(1024)(128)(4,1)S(1)}, s32[]{:S(2)}) async-start(s8[8388608]{0:T(1024)(128)(4,1)} %bitcast.298), calls=%async_computation.4 | async-start | bytes 8388608
  490.1 49.9 %slice-start.1 = ((s8[8388608]{0:T(1024)(128)(4,1)}), s8[4194304]{0:T(1024)(128)(4,1)S(1)}, s32[]{:S(2)}) async-start(s8[8388608]{0:T(1024)(128)(4,1)} %bitcast.298), calls=%async_computation.5 | async-start | bytes 8388608
  540.0 17.1 %copy-start.32 = (f32[4096]{0:T(1024)S(1)}, f32[4096]{0:T(1024)}, u32[]{:S(2)}) copy-start(f32[4096]{0:T(1024)} %copy-done.31) | copy-start | bytes 49156
  557.1 6.3 copy-start.7
  563.5 5.2 copy-start.11
  587.8 12.8 copy-start.16
  725.4 32.6 %copy-start.28 = (f32[4096]{0:T(1024)S(1)}, f32[4096]{0:T(1024)}, u32[]{:S(2)}) copy-start(f32[4096]{0:T(1024)} %div.102) | copy-start | bytes 49156
  725.4 32.6 %copy-start.41 = (f32[512]{0:T(512)S(1)}, f32[512]{0:T(512)}, u32[]{:S(2)}) copy-start(f32[512]{0:T(512)} %param.32) | copy-start | bytes 6148
  725.4 32.6 %copy-start.55 = (bf16[512,1536]{1,0:T(8,128)(2,1)S(1)}, bf16[512,1536]{1,0:T(8,128)(2,1)}, u32[]{:S(2)}) copy-start(bf16[512,1536]{1,0:T(8,128)(2,1)} %param.34) | copy-start | bytes 4718596
  758.0 12.6 copy-start.37
  770.6 6.4 copy-start.8
  770.6 6.4 copy-start.30
  785.6 53.9 %all-to-all-start.2 = ((bf16[1,64,64,512]{3,2,0,1:T(8,128)(2,1)}), bf16[1,64,64,512]{3,2,0,1:T(8,128)(2,1)}, u32[]{:S(2)}, u32[]{:S(2)}) async-start(bf16[1,64,64,512]{3,2,0,1:T(8,128)(2,1)} %bitcast.308), calls=%async_computation.2 | async-start | bytes 8388608 | tf_op jit(solution)/shard_map/all_to_all | solution.py:231
  790.3 12.3 copy-start.9
  839.4 9.4 copy-start.61
  839.4 226.9 %all-to-all-start = ((bf16[1,64,64,512]{3,2,0,1:T(8,128)(2,1)}), bf16[1,64,64,512]{3,2,0,1:T(8,128)(2,1)}, u32[]{:S(2)}, u32[]{:S(2)}) async-start(bf16[1,64,64,512]{3,2,0,1:T(8,128)(2,1)} %bitcast.316), calls=%async_computation | async-start | bytes 8388608 | tf_op jit(solution)/shard_map/all_to_all | solution.py:193
  844.1 500.7 %all-reduce.4.cloned.1.call-start = ((), (), s32[]{:S(2)}) async-start(), calls=%async_computation.3 | async-start | bytes 33554432 | tf_op jit(solution)/shard_map/psum | solution.py:251
  864.5 9.8 copy-start.34
  1043.8 12.9 copy-start.15
  1043.8 12.9 copy-start.14
  1062.2 9.2 copy-start.27
  1062.2 9.1 copy-start.39
  1062.2 9.1 copy-start.57
  1066.3 5.1 copy-start.4
  1084.0 10.6 copy-start.10
  1084.0 10.5 copy-start.43
  1084.0 10.5 copy-start.44
  1084.0 10.5 copy-start.45
  1084.1 10.5 copy-start.49
  1084.1 10.5 copy-start.50
  1084.1 10.5 copy-start.51
  1344.9 6.8 copy-start.22
  1344.9 8.5 copy-start.23
  1344.9 9.4 copy-start.20
  1353.3 5.1 copy-start.1
  (15 other events, 47.5 us)
Sparse Core Ops, SparseCore 0:
  1062.3 282.5 all-reduce.3
